TPU v7x, 128 devices: a whole 4x4x4 slice. The times are simulated.
128 devices in a mesh: expert: 64 (over z, y, x_hi, core), dp: 2 (over x_lo).
Axes of the slice: x: 4 (x_hi: 2, x_lo: 2; x = x_hi * 2 + x_lo), y: 4, z: 4, core: 2. Of those that a mesh axis runs over, the one named last changes fastest.
Arguments:
- tokens: bfloat16 [8192, 4096], P(('expert', 'dp')), may hold values from -6 to 6
- expert_ids: int32 [8192, 8], P(('expert', 'dp')), may hold values from 0 to 127, all different within a row; in each aligned block of 64 rows (0 to 63, 64 to 127, ...) at most 8 rows name the same one
- gate_up: bfloat16 [128, 4096, 1536], P('expert', None, 'dp'), may hold values from -0.09375 to 0.09375
Outputs:
- factors: float32 [128, 768, 768], P('expert', 'dp')
Inputs may be any that keep to these rules, and one draw needn't show every extreme that they name: `expert_ids`: each token names 8 distinct experts. Within each device's aligned block of 64 tokens no expert is named more than 8 times, a bound that some block reaches.
All inputs are finite; a program needn't handle non-finite values.
Results may differ from a plain program's by a relative error of at most 0.004.
Values may be sent and summed in bfloat16 or wider, within the bound.
A program may use at most 192 MiB of HBM per device.

v0:
```python
import jax
import jax.numpy as jnp
from jax import lax
from jax.sharding import PartitionSpec as P

damping = 0.25


def project(rows, weight):
    return jnp.einsum("esd,edc->esc", rows, weight, preferred_element_type=jnp.float32)


def swiglu(both, width):
    return (jax.nn.silu(both[:, :, :width]) * both[:, :, width:]).astype(jnp.bfloat16)


def second_moment(hidden, scale, extra):
    gram = jnp.einsum("esf,esg->efg", hidden, hidden, preferred_element_type=jnp.float32)
    identity = jnp.eye(hidden.shape[2], dtype=jnp.float32)
    return gram * scale + extra * identity[None]


def upper_factor(moment):
    return jnp.swapaxes(jnp.linalg.cholesky(moment), 1, 2)


def on_device(tokens, expert_ids, gate_up):
    expert_axis = lax.axis_size("expert")
    replicas = lax.axis_size("dp")
    local_count = gate_up.shape[0]
    expert_count = local_count * expert_axis
    token_count, top_count = expert_ids.shape
    width_full = gate_up.shape[2] * replicas // 2
    width_part = width_full // replicas
    capacity = 2 * token_count * top_count // expert_count
    rows_mean = token_count * expert_axis * replicas * top_count // expert_count
    scale = 1.0 / rows_mean
    extra = damping * damping / replicas
    flat_ids = expert_ids.reshape(-1)
    onehot = (flat_ids[:, None] == jnp.arange(expert_count, dtype=jnp.int32)[None, :]).astype(
        jnp.int32
    )
    ranking = jnp.sum((jnp.cumsum(onehot, axis=0) - 1) * onehot, axis=1)
    target = flat_ids * capacity + ranking
    placing = jnp.arange(expert_count * capacity, dtype=jnp.int32)[:, None] == target[None, :]
    placing = jnp.any(
        placing.reshape(expert_count * capacity, token_count, top_count), axis=2
    ).astype(jnp.bfloat16)
    outgoing = jnp.dot(placing, tokens, preferred_element_type=jnp.float32).astype(jnp.bfloat16)
    outgoing = outgoing.reshape(expert_count, capacity, tokens.shape[1])
    arrived = lax.all_to_all(outgoing, "expert", split_axis=0, concat_axis=1, tiled=True)
    both = project(arrived, lax.all_gather(gate_up, "dp", axis=2, tiled=True))
    hidden = swiglu(both, width_full)
    local_moment = second_moment(hidden, scale, extra)
    total_moment = lax.psum(local_moment, "dp")
    factor = upper_factor(total_moment)
    position = lax.axis_index("dp")
    return lax.dynamic_slice_in_dim(factor, position * width_part, width_part, 1)


def solution(mesh):
    return jax.shard_map(
        on_device,
        mesh=mesh,
        in_specs=(P(("expert", "dp"), None), P(("expert", "dp"), None), P("expert", None, "dp")),
        out_specs=P("expert", "dp", None),
        check_vma=False,
    )
```

profile of v0, /device:TPU:1, one launch (start us, length us, event | category | flops | bytes accessed | tf_op | source)
XLA Modules:
  0.0 836.7 jit_solution(10531696009400579675)
XLA Ops:
  6.5 0.7 all-gather.2.cloned.1.call-update
  7.7 0.2 fusion.23
  8.0 0.2 fusion.22
  8.5 0.7 fusion.8
  9.2 5.6 convert_bitcast_fusion
  14.8 12.7 %all-to-all-start = ((bf16[128,8,4096]{2,1,0:T(8,128)(2,1)}), bf16[128,8,4096]{2,1,0:T(8,128)(2,1)}, u32[]{:S(2)}, u32[]{:S(2)}) async-start(bf16[128,8,4096]{2,1,0:T(8,128)(2,1)} %convert_bitcast_fusion), calls=%async_computation | async-start | bytes 16777216 | tf_op jit(solution)/shard_map/all_to_all | solution.py:51
  27.5 0.2 all-reduce.3.cloned.1.call-start
  27.7 0.2 fusion.7
  27.9 176.4 %all-to-all-done = bf16[128,8,4096]{2,1,0:T(8,128)(2,1)} async-done(((bf16[128,8,4096]{2,1,0:T(8,128)(2,1)}), bf16[128,8,4096]{2,1,0:T(8,128)(2,1)}, u32[]{:S(2)}, u32[]{:S(2)}) %all-to-all-start) | async-done | bytes 8388640 | tf_op jit(solution)/shard_map/all_to_all | solution.py:51
  204.2 184.2 %all-gather.2.cloned.1.call-done = bf16[2,4096,1536]{2,1,0:T(8,128)(2,1)} async-done(((bf16[2,4096,768]{2,1,0:T(8,128)(2,1)}), bf16[2,4096,1536]{2,1,0:T(8,128)(2,1)}) %all-gather.2.cloned.1.call-update) | async-done | bytes 25165840 | tf_op jit(solution)/shard_map/all_gather | solution.py:52
  388.4 20.7 %fusion = f32[2,512,1536]{2,1,0:T(8,128)} fusion(bf16[2,4096,1536]{2,1,0:T(8,128)(2,1)} %all-gather.2.cloned.1.call-done, bf16[64,2,8,4096]{3,2,1,0:T(8,128)(2,1)} %bitcast.4), kind=kOutput, calls=%fused_computation | convolution fusion | flops 12884901888 | bytes 39845888 | tf_op jit(solution)/shard_map/esd,edc->esc/dot_general | solution.py:10
  409.2 9.1 %multiply_add_fusion = f32[2,768,768]{1,2,0:T(8,128)} fusion(f32[768,768]{0,1:T(8,128)S(1)} %fusion.7, f32[2,512,1536]{2,1,0:T(8,128)} %fusion), kind=kOutput, calls=%fused_computation.6 | convolution fusion | flops 1215037440 | bytes 13369344 | tf_op jit(solution)/shard_map/esf,esg->efg/dot_general | solution.py:18
  418.4 0.2 iota_compare_fusion.1
  418.6 128.3 %all-reduce.3.cloned.1.call-done = f32[2,768,768]{1,2,0:T(8,128)} async-done(((f32[2,768,768]{1,2,0:T(8,128)}), f32[2,768,768]{1,2,0:T(8,128)}) %all-reduce.3.cloned.1.call-update) | async-done | bytes 4718608 | tf_op jit(solution)/shard_map/psum | solution.py:55
  546.9 6.2 copy.71
  553.1 4.4 fusion.3
  557.4 2.1 copy-done.2
  559.6 23.5 %custom-call.49 = f32[2,128,128]{2,1,0:T(8,128)S(1)} custom-call(f32[2,128,128]{2,1,0:T(8,128)S(1)} %cholesky.426), custom_call_target="Cholesky" | custom-call | tf_op jit(solution)/shard_map/jit(cholesky)/cholesky | solution.py:24
  583.1 19.9 %custom-call.50 = f32[2,1,128,128]{2,3,1,0:T(8,128)S(1)} custom-call(f32[2,1,128,128]{3,2,1,0:T(8,128)S(1)} %select_bitcast_fusion.4), custom_call_target="InvertDiagBlocksLowerTriangular" | custom-call | tf_op jit(solution)/shard_map/jit(cholesky)/cholesky | solution.py:24
  602.9 2.5 cholesky.197
  605.4 2.8 constant_dynamic-update-slice_fusion.5
  608.2 1.8 convolution_subtract_fusion
  610.0 23.5 %custom-call.51 = f32[2,128,128]{2,1,0:T(8,128)S(1)} custom-call(f32[2,128,128]{2,1,0:T(8,128)S(1)} %cholesky.430), custom_call_target="Cholesky" | custom-call | tf_op jit(solution)/shard_map/jit(cholesky)/cholesky | solution.py:24
  633.5 0.7 select_bitcast_fusion.3
  634.2 19.7 %custom-call.52 = f32[2,1,128,128]{2,3,1,0:T(8,128)S(1)} custom-call(f32[2,1,128,128]{3,2,1,0:T(8,128)S(1)} %get-tuple-element.18), custom_call_target="InvertDiagBlocksLowerTriangular" | custom-call | tf_op jit(solution)/shard_map/jit(cholesky)/cholesky | solution.py:24
  653.9 1.4 convolution_dynamic-update-slice_fusion
  655.3 2.5 convolution_subtract_fusion.1
  657.9 23.9 %custom-call.53 = f32[2,128,128]{2,1,0:T(8,128)S(1)} custom-call(f32[2,128,128]{2,1,0:T(8,128)S(1)} %cholesky.435), custom_call_target="Cholesky" | custom-call | tf_op jit(solution)/shard_map/jit(cholesky)/cholesky | solution.py:24
  681.7 0.7 select_bitcast_fusion.2
  682.4 19.7 %custom-call.54 = f32[2,1,128,128]{2,3,1,0:T(8,128)S(1)} custom-call(f32[2,1,128,128]{3,2,1,0:T(8,128)S(1)} %get-tuple-element.16), custom_call_target="InvertDiagBlocksLowerTriangular" | custom-call | tf_op jit(solution)/shard_map/jit(cholesky)/cholesky | solution.py:24
  702.1 1.3 convolution_dynamic-update-slice_fusion.1
  703.4 2.7 convolution_subtract_fusion.2
  706.1 23.5 %custom-call.55 = f32[2,128,128]{2,1,0:T(8,128)S(1)} custom-call(f32[2,128,128]{2,1,0:T(8,128)S(1)} %cholesky.440), custom_call_target="Cholesky" | custom-call | tf_op jit(solution)/shard_map/jit(cholesky)/cholesky | solution.py:24
  729.6 0.7 select_bitcast_fusion.1
  730.3 19.8 %custom-call.56 = f32[2,1,128,128]{2,3,1,0:T(8,128)S(1)} custom-call(f32[2,1,128,128]{3,2,1,0:T(8,128)S(1)} %get-tuple-element.14), custom_call_target="InvertDiagBlocksLowerTriangular" | custom-call | tf_op jit(solution)/shard_map/jit(cholesky)/cholesky | solution.py:24
  750.1 1.1 convolution_dynamic-update-slice_fusion.2
  751.2 2.5 convolution_subtract_fusion.3
  753.8 23.5 %custom-call.57 = f32[2,128,128]{2,1,0:T(8,128)S(1)} custom-call(f32[2,128,128]{2,1,0:T(8,128)S(1)} %cholesky.445), custom_call_target="Cholesky" | custom-call | tf_op jit(solution)/shard_map/jit(cholesky)/cholesky | solution.py:24
  777.2 0.7 select_bitcast_fusion
  777.9 19.7 %custom-call.58 = f32[2,1,128,128]{2,3,1,0:T(8,128)S(1)} custom-call(f32[2,1,128,128]{3,2,1,0:T(8,128)S(1)} %get-tuple-element.12), custom_call_target="InvertDiagBlocksLowerTriangular" | custom-call | tf_op jit(solution)/shard_map/jit(cholesky)/cholesky | solution.py:24
  797.6 0.9 convolution_dynamic-update-slice_fusion.3
  798.5 2.2 convolution_subtract_fusion.4
  800.7 23.7 %custom-call.59 = f32[2,128,128]{2,1,0:T(8,128)S(1)} custom-call(f32[2,128,128]{2,1,0:T(8,128)S(1)} %convolution_subtract_fusion.4), custom_call_target="Cholesky" | custom-call | tf_op jit(solution)/shard_map/jit(cholesky)/cholesky | solution.py:24
  824.4 0.7 select_reduce_fusion.4
  825.3 0.2 compare_reduce_fusion.2
  825.4 0.2 compare_reduce_fusion
  825.6 2.1 fusion.6
  827.7 2.0 copy.82
  (33 shorter events, 1.1 us)
Async XLA Ops:
  6.5 2.7 copy-start
  6.5 0.7 copy-start.3
  6.5 381.9 %all-gather.2.cloned.1.call-start = ((), (), s32[]{:S(2)}) async-start(), calls=%async_computation.1 | async-start | bytes 37748736 | tf_op jit(solution)/shard_map/all_gather | solution.py:52
  14.8 189.4 %all-to-all-start = ((bf16[128,8,4096]{2,1,0:T(8,128)(2,1)}), bf16[128,8,4096]{2,1,0:T(8,128)(2,1)}, u32[]{:S(2)}, u32[]{:S(2)}) async-start(bf16[128,8,4096]{2,1,0:T(8,128)(2,1)} %convert_bitcast_fusion), calls=%async_computation | async-start | bytes 16777216 | tf_op jit(solution)/shard_map/all_to_all | solution.py:51
  27.5 519.4 %all-reduce.3.cloned.1.call-start = ((), (), s32[]{:S(2)}) async-start(), calls=%async_computation.2 | async-start | bytes 9437184 | tf_op jit(solution)/shard_map/psum | solution.py:55
  557.4 2.1 copy-start.2
  825.6 4.1 copy-start.1
Sparse Core Ops, SparseCore 0:
  9.0 379.3 all-gather.1
  418.4 128.4 all-reduce.2
where the time goes:
time: 841 us; the launch traced here: 837 us
  waiting for transfers between devices  490 us (58%)
  other arithmetic  252 us (30%)
  matrix products  54.7 us (7%)
  between operations  13.9 us (2%)
  local copies, waits for them, and re-layouts  13.5 us (2%)
  starting transfers between devices  12.9 us (2%)
    another operation x23, other arithmetic, upper_factor(): return jnp.swapaxes(jnp.linalg.cholesky(moment), 1, 2)  244 us
    all_gather x1, waiting for transfers between devices, on_device(): both = project(arrived, lax.all_gather(gate_up, 'dp', axis=2, tiled=True))  184 us
    all_to_all x1, waiting for transfers between devices, on_device(): lax.all_to_all(outgoing, 'expert', split_axis=0, concat_axis=1, tiled=True)  176 us
    psum x1, waiting for transfers between devices, on_device(): total_moment = lax.psum(local_moment, 'dp')  128 us
    dot_general x1, matrix products, project(): jnp.einsum('esd,edc->esc', rows, weight, preferred_element_type=jnp.float32)  20.7 us
    another operation x10, matrix products, upper_factor(): return jnp.swapaxes(jnp.linalg.cholesky(moment), 1, 2)  19.3 us
  transfers between devices with their start and end apart: 3, of which 3 were waited for; matrix products, arithmetic and copies ran while one was open for 1% of the time, Pallas kernels for 0%

commit v1 on v0

--- a/solution.py
+++ b/solution.py
@@ -49,7 +49,12 @@
     outgoing = jnp.dot(placing, tokens, preferred_element_type=jnp.float32).astype(jnp.bfloat16)
     outgoing = outgoing.reshape(expert_count, capacity, tokens.shape[1])
     arrived = lax.all_to_all(outgoing, "expert", split_axis=0, concat_axis=1, tiled=True)
-    both = project(arrived, lax.all_gather(gate_up, "dp", axis=2, tiled=True))
+    both = project(
+        arrived,
+        jnp.concatenate(
+            lax.all_to_all(jnp.stack([gate_up] * lax.axis_size("dp")), "dp", 0, 0), axis=2
+        ),
+    )
     hidden = swiglu(both, width_full)
     local_moment = second_moment(hidden, scale, extra)
     total_moment = lax.psum(local_moment, "dp")

time: 841 us -> 889 us (1.057)
  other arithmetic: 252 us -> 273 us
  local copies, waits for them, and re-layouts: 13.5 us -> 34.5 us
  starting transfers between devices: 12.9 us -> 25.5 us
    all_to_all x0 -> x1, waiting for transfers between devices: none -> 264 us  [on_device(): lax.all_to_all(jnp.stack([gate_up] * lax.axis_size('dp')), 'dp', 0, 0)]
    all_gather x1 -> x0, waiting for transfers between devices: 184 us -> none  [on_device(): both = project(arrived, lax.all_gather(gate_up, 'dp', axis=2, tiled=True))]
    all_to_all x1, waiting for transfers between devices: 176 us -> 78.5 us  [on_device(): lax.all_to_all(outgoing, 'expert', split_axis=0, concat_axis=1, tiled=True)]
    reshape x0 -> x1, local copies, waits for them, and re-layouts: none -> 21 us  [on_device(): jnp.concatenate(lax.all_to_all(jnp.stack([gate_up] * lax.axis_size('dp'))...]
    another operation x2 -> x3, other arithmetic: 0.24 us -> 21 us  [the longest x1 20.8 us: on_device(): jnp.stack([gate_up] * lax.axis_size('dp'))]
    all_to_all x0 -> x1, starting transfers between devices: none -> 11.9 us  [on_device(): lax.all_to_all(jnp.stack([gate_up] * lax.axis_size('dp')), 'dp', 0, 0)]
    psum x1, waiting for transfers between devices: 128 us -> 140 us  [on_device(): total_moment = lax.psum(local_moment, 'dp')]
  transfers between devices with their start and end apart: 3 -> 3, of which waited for: 3 -> 3; matrix products, arithmetic and copies ran while one was open for 1% -> 3% of each run, Pallas kernels for 0% -> 0%
where the time goes in v1:
time: 889 us; the launch traced here: 884 us
  waiting for transfers between devices  483 us (54%)
  other arithmetic  273 us (31%)
  matrix products  54.7 us (6%)
  local copies, waits for them, and re-layouts  34.5 us (4%)
  starting transfers between devices  25.5 us (3%)
  between operations  13.9 us (2%)
    all_to_all x1, waiting for transfers between devices, on_device(): lax.all_to_all(jnp.stack([gate_up] * lax.axis_size('dp')), 'dp', 0, 0)  264 us
    another operation x23, other arithmetic, upper_factor(): return jnp.swapaxes(jnp.linalg.cholesky(moment), 1, 2)  244 us
    psum x1, waiting for transfers between devices, on_device(): total_moment = lax.psum(local_moment, 'dp')  140 us
    all_to_all x1, waiting for transfers between devices, on_device(): lax.all_to_all(outgoing, 'expert', split_axis=0, concat_axis=1, tiled=True)  78.5 us
    reshape x1, local copies, waits for them, and re-layouts, on_device(): jnp.concatenate(lax.all_to_all(jnp.stack([gate_up] * lax.axis_size('dp'))...  21 us
    another operation x1, other arithmetic, on_device(): jnp.stack([gate_up] * lax.axis_size('dp'))  20.8 us
    dot_general x1, matrix products, project(): jnp.einsum('esd,edc->esc', rows, weight, preferred_element_type=jnp.float32)  20.6 us
    another operation x10, matrix products, upper_factor(): return jnp.swapaxes(jnp.linalg.cholesky(moment), 1, 2)  19.3 us
  transfers between devices with their start and end apart: 3, of which 3 were waited for; matrix products, arithmetic and copies ran while one was open for 3% of the time, Pallas kernels for 0%

profile of v1, /device:TPU:1, one launch (start us, length us, event | category | flops | bytes accessed | tf_op | source)
XLA Modules:
  0.0 884.3 jit_solution(2649171574555066523)
XLA Ops:
  6.5 20.8 %pad_maximum_fusion = bf16[2,2,4096,768]{3,2,1,0:T(8,128)(2,1)} fusion(bf16[1,2,4096,768]{3,2,1,0:T(8,128)(2,1)} %bitcast.68), kind=kLoop, calls=%fused_computation | loop fusion | flops 12582912 | bytes 37748736 | tf_op jit(solution)/shard_map/stack | solution.py:55
  27.3 11.9 %all-to-all-start.1 = ((bf16[2,2,4096,768]{3,2,1,0:T(8,128)(2,1)}), bf16[2,2,4096,768]{3,2,1,0:T(8,128)(2,1)}, u32[]{:S(2)}, u32[]{:S(2)}) async-start(bf16[2,2,4096,768]{3,2,1,0:T(8,128)(2,1)} %pad_maximum_fusion), calls=%async_computation.1 | async-start | bytes 50331648 | tf_op jit(solution)/shard_map/all_to_all | solution.py:55
  39.6 0.2 fusion.23
  40.0 0.2 fusion.22
  40.5 0.7 fusion.8
  41.2 5.6 convert_bitcast_fusion
  46.8 264.1 %all-to-all-done.1 = bf16[2,2,4096,768]{3,2,1,0:T(8,128)(2,1)} async-done(((bf16[2,2,4096,768]{3,2,1,0:T(8,128)(2,1)}), bf16[2,2,4096,768]{3,2,1,0:T(8,128)(2,1)}, u32[]{:S(2)}, u32[]{:S(2)}) %all-to-all-start.1) | async-done | bytes 25165856 | tf_op jit(solution)/shard_map/all_to_all | solution.py:55
  310.9 13.3 %all-to-all-start = ((bf16[128,8,4096]{2,1,0:T(8,128)(2,1)}), bf16[128,8,4096]{2,1,0:T(8,128)(2,1)}, u32[]{:S(2)}, u32[]{:S(2)}) async-start(bf16[128,8,4096]{2,1,0:T(8,128)(2,1)} %convert_bitcast_fusion), calls=%async_computation | async-start | bytes 16777216 | tf_op jit(solution)/shard_map/all_to_all | solution.py:51
  324.3 0.2 all-reduce.3.cloned.1.call-start
  324.5 0.2 fusion.7
  324.7 21.0 %copy.94 = bf16[2,2,512,8,768]{4,3,0,2,1:T(8,128)(2,1)} copy(bf16[2,2,512,8,768]{4,3,2,1,0:T(8,128)(2,1)} %bitcast.33) | data formatting | bytes 50331648 | tf_op jit(solution)/shard_map/reshape | solution.py:54
  345.6 78.5 %all-to-all-done = bf16[128,8,4096]{2,1,0:T(8,128)(2,1)} async-done(((bf16[128,8,4096]{2,1,0:T(8,128)(2,1)}), bf16[128,8,4096]{2,1,0:T(8,128)(2,1)}, u32[]{:S(2)}, u32[]{:S(2)}) %all-to-all-start) | async-done | bytes 8388640 | tf_op jit(solution)/shard_map/all_to_all | solution.py:51
  424.1 20.6 %fusion = f32[2,512,1536]{2,1,0:T(8,128)} fusion(bf16[2,4096,1536]{2,1,0:T(8,128)(2,1)} %bitcast.67, bf16[64,2,8,4096]{3,2,1,0:T(8,128)(2,1)} %bitcast.4), kind=kOutput, calls=%fused_computation.1 | convolution fusion | flops 12884901888 | bytes 39845888 | tf_op jit(solution)/shard_map/esd,edc->esc/dot_general | solution.py:10
  444.7 9.2 %multiply_add_fusion = f32[2,768,768]{1,2,0:T(8,128)} fusion(f32[768,768]{0,1:T(8,128)S(1)} %fusion.7, f32[2,512,1536]{2,1,0:T(8,128)} %fusion), kind=kOutput, calls=%fused_computation.7 | convolution fusion | flops 1215037440 | bytes 13369344 | tf_op jit(solution)/shard_map/esf,esg->efg/dot_general | solution.py:18
  454.0 0.2 iota_compare_fusion.1
  454.3 140.2 %all-reduce.3.cloned.1.call-done = f32[2,768,768]{1,2,0:T(8,128)} async-done(((f32[2,768,768]{1,2,0:T(8,128)}), f32[2,768,768]{1,2,0:T(8,128)}) %all-reduce.3.cloned.1.call-update) | async-done | bytes 4718608 | tf_op jit(solution)/shard_map/psum | solution.py:60
  594.4 6.2 copy.75
  600.6 4.4 fusion.3
  605.0 2.1 copy-done.2
  607.1 23.5 %custom-call.49 = f32[2,128,128]{2,1,0:T(8,128)S(1)} custom-call(f32[2,128,128]{2,1,0:T(8,128)S(1)} %cholesky.426), custom_call_target="Cholesky" | custom-call | tf_op jit(solution)/shard_map/jit(cholesky)/cholesky | solution.py:24
  630.6 2.5 cholesky.197
  633.1 19.9 %custom-call.50 = f32[2,1,128,128]{2,3,1,0:T(8,128)S(1)} custom-call(f32[2,1,128,128]{3,2,1,0:T(8,128)S(1)} %select_bitcast_fusion.4), custom_call_target="InvertDiagBlocksLowerTriangular" | custom-call | tf_op jit(solution)/shard_map/jit(cholesky)/cholesky | solution.py:24
  653.0 2.8 constant_dynamic-update-slice_fusion.5
  655.8 1.8 convolution_subtract_fusion
  657.6 23.5 %custom-call.51 = f32[2,128,128]{2,1,0:T(8,128)S(1)} custom-call(f32[2,128,128]{2,1,0:T(8,128)S(1)} %cholesky.430), custom_call_target="Cholesky" | custom-call | tf_op jit(solution)/shard_map/jit(cholesky)/cholesky | solution.py:24
  681.0 0.7 select_bitcast_fusion.3
  681.8 19.7 %custom-call.52 = f32[2,1,128,128]{2,3,1,0:T(8,128)S(1)} custom-call(f32[2,1,128,128]{3,2,1,0:T(8,128)S(1)} %get-tuple-element.18), custom_call_target="InvertDiagBlocksLowerTriangular" | custom-call | tf_op jit(solution)/shard_map/jit(cholesky)/cholesky | solution.py:24
  701.4 1.4 convolution_dynamic-update-slice_fusion
  702.9 2.5 convolution_subtract_fusion.1
  705.4 23.9 %custom-call.53 = f32[2,128,128]{2,1,0:T(8,128)S(1)} custom-call(f32[2,128,128]{2,1,0:T(8,128)S(1)} %cholesky.435), custom_call_target="Cholesky" | custom-call | tf_op jit(solution)/shard_map/jit(cholesky)/cholesky | solution.py:24
  729.3 0.7 select_bitcast_fusion.2
  730.0 19.7 %custom-call.54 = f32[2,1,128,128]{2,3,1,0:T(8,128)S(1)} custom-call(f32[2,1,128,128]{3,2,1,0:T(8,128)S(1)} %get-tuple-element.16), custom_call_target="InvertDiagBlocksLowerTriangular" | custom-call | tf_op jit(solution)/shard_map/jit(cholesky)/cholesky | solution.py:24
  749.6 1.3 convolution_dynamic-update-slice_fusion.1
  751.0 2.7 convolution_subtract_fusion.2
  753.7 23.5 %custom-call.55 = f32[2,128,128]{2,1,0:T(8,128)S(1)} custom-call(f32[2,128,128]{2,1,0:T(8,128)S(1)} %cholesky.440), custom_call_target="Cholesky" | custom-call | tf_op jit(solution)/shard_map/jit(cholesky)/cholesky | solution.py:24
  777.1 0.7 select_bitcast_fusion.1
  777.8 19.8 %custom-call.56 = f32[2,1,128,128]{2,3,1,0:T(8,128)S(1)} custom-call(f32[2,1,128,128]{3,2,1,0:T(8,128)S(1)} %get-tuple-element.14), custom_call_target="InvertDiagBlocksLowerTriangular" | custom-call | tf_op jit(solution)/shard_map/jit(cholesky)/cholesky | solution.py:24
  797.7 1.1 convolution_dynamic-update-slice_fusion.2
  798.8 2.5 convolution_subtract_fusion.3
  801.3 23.5 %custom-call.57 = f32[2,128,128]{2,1,0:T(8,128)S(1)} custom-call(f32[2,128,128]{2,1,0:T(8,128)S(1)} %cholesky.445), custom_call_target="Cholesky" | custom-call | tf_op jit(solution)/shard_map/jit(cholesky)/cholesky | solution.py:24
  824.8 0.7 select_bitcast_fusion
  825.5 19.7 %custom-call.58 = f32[2,1,128,128]{2,3,1,0:T(8,128)S(1)} custom-call(f32[2,1,128,128]{3,2,1,0:T(8,128)S(1)} %get-tuple-element.12), custom_call_target="InvertDiagBlocksLowerTriangular" | custom-call | tf_op jit(solution)/shard_map/jit(cholesky)/cholesky | solution.py:24
  845.1 0.9 convolution_dynamic-update-slice_fusion.3
  846.1 2.2 convolution_subtract_fusion.4
  848.2 23.7 %custom-call.59 = f32[2,128,128]{2,1,0:T(8,128)S(1)} custom-call(f32[2,128,128]{2,1,0:T(8,128)S(1)} %convolution_subtract_fusion.4), custom_call_target="Cholesky" | custom-call | tf_op jit(solution)/shard_map/jit(cholesky)/cholesky | solution.py:24
  871.9 0.7 select_reduce_fusion.4
  873.1 2.1 fusion.6
  875.2 2.0 copy.86
  (34 shorter events, 1.4 us)
Async XLA Ops:
  6.5 34.6 %copy-start = (bf16[64,4096]{1,0:T(8,128)(2,1)S(1)}, bf16[64,4096]{1,0:T(8,128)(2,1)}, u32[]{:S(2)}) copy-start(bf16[64,4096]{1,0:T(8,128)(2,1)} %param.3) | copy-start | bytes 1572868
  27.3 11.9 %copy-start.3 = (s32[64,8]{0,1:T(8,128)S(1)}, s32[64,8]{0,1:T(8,128)}, u32[]{:S(2)}) copy-start(s32[64,8]{0,1:T(8,128)} %param.4) | copy-start | bytes 6148
  27.3 283.6 %all-to-all-start.1 = ((bf16[2,2,4096,768]{3,2,1,0:T(8,128)(2,1)}), bf16[2,2,4096,768]{3,2,1,0:T(8,128)(2,1)}, u32[]{:S(2)}, u32[]{:S(2)}) async-start(bf16[2,2,4096,768]{3,2,1,0:T(8,128)(2,1)} %pad_maximum_fusion), calls=%async_computation.1 | async-start | bytes 50331648 | tf_op jit(solution)/shard_map/all_to_all | solution.py:55
  310.9 113.2 %all-to-all-start = ((bf16[128,8,4096]{2,1,0:T(8,128)(2,1)}), bf16[128,8,4096]{2,1,0:T(8,128)(2,1)}, u32[]{:S(2)}, u32[]{:S(2)}) async-start(bf16[128,8,4096]{2,1,0:T(8,128)(2,1)} %convert_bitcast_fusion), calls=%async_computation | async-start | bytes 16777216 | tf_op jit(solution)/shard_map/all_to_all | solution.py:51
  324.3 270.2 %all-reduce.3.cloned.1.call-start = ((), (), s32[]{:S(2)}) async-start(), calls=%async_computation.2 | async-start | bytes 9437184 | tf_op jit(solution)/shard_map/psum | solution.py:60
  605.0 2.1 copy-start.2
  873.1 4.1 copy-start.1
Sparse Core Ops, SparseCore 0:
  454.1 140.3 all-reduce.2
